TPU v7x, 32 devices: a whole 2x2x4 slice. The times are simulated.
32 devices in a mesh: rows: 16 (over z, x, core), cols: 2 (over y).
Axes of the slice: x: 2, y: 2, z: 4, core: 2. Of those that a mesh axis runs over, the one named last changes fastest.
Arguments:
- unfolding: float32 [8192, 4096], P('rows', 'cols'), may hold values from -6 to 6
- pattern: int32 [32, 2], P('cols'), may hold values from 0 to 1, as said below
- sign_bits: int32 [4096, 2], P('cols'), may hold values from 0 to 1
Outputs:
- core_scaled: float32 [8192, 256], P('rows')
- next_unfolding: float32 [2048, 512], P('rows', 'cols')
Inputs may be any that keep to these rules, and one draw needn't show every extreme that they name: Every row and every column of pattern holds at least one 1, and some entry is 0.
All inputs are finite; a program needn't handle non-finite values.
Results may differ from a plain program's by a relative error of at most 0.00017.
Values sent between devices are 32-bit elements; how exact they have to be, the bound alone decides.
No kernel may reach another device: no remote copies, remote signals or barrier semaphores. Data moves between devices by JAX's collectives and lax.ppermute only.
A program may use at most 64 MiB of HBM per device.

v0:
```python
import math
import jax
import jax.numpy as jnp
from jax import lax
from jax.sharding import PartitionSpec as P

RANK = 256
BLK = 128
MODE = 8


def hadamard_table(table_size):
    row_index = lax.broadcasted_iota(jnp.int32, (table_size, table_size), 0)
    col_index = lax.broadcasted_iota(jnp.int32, (table_size, table_size), 1)
    parity = jnp.zeros((table_size, table_size), jnp.int32)
    for bit_level in range(table_size.bit_length() - 1):
        bit_value = 1 << bit_level
        parity = parity + row_index // bit_value % 2 * (col_index // bit_value % 2)
    return (1 - 2 * (parity % 2)).astype(jnp.float32)


def sketch_matrix(pattern, sign_bits, block_size):
    blocks = sign_bits.shape[1]
    rows_here = sign_bits.shape[0]
    hadamard = hadamard_table(block_size)
    factor = jnp.repeat(pattern, block_size, axis=0) * (2 * sign_bits - 1)
    tiled_table = jnp.tile(hadamard, (rows_here // block_size, 1))
    expanded = factor.astype(jnp.float32)[:, :, None] * tiled_table[:, None, :]
    return expanded.reshape(rows_here, blocks * block_size)


def inner_rows(left_side, right_side):
    return lax.dot_general(
        left_side, right_side, (((0,), (0,)), ((), ())), precision=lax.Precision.HIGHEST
    )


def local(unfolding, pattern, sign_bits):
    highest = lax.Precision.HIGHEST
    sketch_map = sketch_matrix(pattern, sign_bits, BLK)
    local_rows = unfolding.shape[0]
    local_cols = unfolding.shape[1]
    row_devices = lax.axis_size("rows")
    col_devices = lax.axis_size("cols")
    total_rows = local_rows * row_devices
    partial_sketch = jnp.dot(unfolding, sketch_map, precision=highest)
    sketch = lax.psum(partial_sketch, "cols")
    gram_matrix = lax.psum(inner_rows(sketch, sketch), "rows")
    gram_matrix = gram_matrix + float(total_rows) * jnp.eye(RANK, dtype=jnp.float32)
    lower_factor = jnp.linalg.cholesky(gram_matrix)
    basis_rows = lax.linalg.triangular_solve(
        lower_factor, sketch, left_side=False, lower=True, transpose_a=True
    )
    core_scaled = basis_rows * math.sqrt(total_rows)
    mode_local = MODE // col_devices
    rest_cols = local_cols // mode_local
    rank_share = RANK // row_devices
    reduced = lax.psum_scatter(
        inner_rows(basis_rows, unfolding), "rows", scatter_dimension=0, tiled=True
    )
    grouped = reduced.reshape(rank_share, mode_local, rest_cols)
    regrouped = lax.all_to_all(grouped, "cols", split_axis=2, concat_axis=1, tiled=True)
    next_unfolding = regrouped.reshape(rank_share * MODE, regrouped.shape[2])
    return (core_scaled, next_unfolding)


def solution(mesh):
    in_specs = (P("rows", "cols"), P("cols", None), P("cols", None))
    out_specs = (P("rows", None), P("rows", "cols"))
    return jax.shard_map(local, mesh=mesh, in_specs=in_specs, out_specs=out_specs, check_vma=False)
```

profile of v0, /device:TPU:0, one launch (start us, length us, event | category | flops | bytes accessed | tf_op | source)
XLA Modules:
  0.0 304.2 jit_solution(9669718208111324517)
XLA Ops:
  7.3 0.5 copy-done
  7.9 0.7 fusion.51
  8.7 0.4 copy.24
  9.0 0.4 fusion.27
  9.4 0.1 tile.8
  9.5 7.7 %broadcast_multiply_fusion = f32[2048,2,128]{2,1,0:T(2,128)S(1)} fusion(f32[2048,128]{1,0:T(8,128)S(1)} %bitcast.58, f32[2048,2]{1,0:T(8,128)S(1)} %copy.24), kind=kLoop, calls=%fused_computation.8 | loop fusion | flops 524288 | bytes 3162112 | tf_op jit(solution)/shard_map/mul | solution.py:28
  17.3 8.1 %fusion.3 = f32[512,256]{0,1:T(8,128)} fusion(f32[512,2048]{1,0:T(8,128)S(1)} %copy-done.1, f32[256,8,2,128]{3,2,1,0:T(2,128)S(1)} %bitcast.55), kind=kOutput, calls=%fused_computation.5 | convolution fusion | flops 3221225472 | bytes 6815744 | tf_op jit(solution)/shard_map/dot_general | solution.py:46
  25.5 31.4 %all-reduce.4.cloned.1.call-done = f32[512,256]{0,1:T(8,128)} async-done(((f32[512,256]{0,1:T(8,128)}), f32[512,256]{0,1:T(8,128)}) %all-reduce.4.cloned.1.call-update) | async-done | bytes 524304 | tf_op jit(solution)/shard_map/psum | solution.py:47
  56.9 2.5 fusion.55
  59.4 0.2 reduce-scatter.2.cloned.1.call-start
  59.7 90.3 %all-reduce.6.cloned.1.call-done = f32[256,256]{0,1:T(8,128)} async-done(((f32[256,256]{0,1:T(8,128)}), f32[256,256]{0,1:T(8,128)}) %all-reduce.6.cloned.1.call-update) | async-done | bytes 262160 | tf_op jit(solution)/shard_map/psum | solution.py:48
  150.0 1.0 select_add_fusion
  150.9 0.1 copy.26
  151.1 1.0 fusion.10
  152.1 11.7 %cholesky.45 = f32[128,128]{1,0:T(8,128)S(1)} custom-call(f32[128,128]{1,0:T(8,128)S(1)} %cholesky.107), custom_call_target="Cholesky" | custom-call | tf_op jit(solution)/shard_map/jit(cholesky)/cholesky | solution.py:50
  163.8 9.8 %custom-call.14 = f32[1,128,128]{1,2,0:T(8,128)S(1)} custom-call(f32[1,128,128]{2,1,0:T(8,128)S(1)} %get-tuple-element.39), custom_call_target="InvertDiagBlocksLowerTriangular" | custom-call | tf_op jit(solution)/shard_map/jit(cholesky)/cholesky | solution.py:50
  173.7 0.2 fusion.42
  173.9 0.3 convolution_subtract_fusion.1
  174.1 11.7 %cholesky.95 = f32[128,128]{1,0:T(8,128)S(1)} custom-call(f32[128,128]{1,0:T(8,128)S(1)} %convolution_subtract_fusion.1), custom_call_target="Cholesky" | custom-call | tf_op jit(solution)/shard_map/jit(cholesky)/cholesky | solution.py:50
  185.9 0.1 copy.29
  186.0 0.1 copy.28
  186.1 0.1 copy.27
  186.2 0.7 compare_reduce_fusion
  186.9 0.6 compare_reduce_fusion.1
  188.9 4.3 %while.1 = (s32[]{:T(128)}, f32[256,256]{0,1:T(8,128)S(1)}, s32[2,2]{1,0:T(2,128)S(1)}, f32[2,128,128]{2,1,0:T(8,128)S(1)}, s32[]{:T(128)}) while((s32[]{:T(128)}, f32[256,256]{0,1:T(8,128)S(1)}, s32[2,2]{1,0:T(2,128)S(1)}, f32[2,128,128]{2,1,0:T(8,128)S(1)}, s32[]{:T(128)}) %tuple.39), condition=%wide.while_cond, body=%wide.while_body.sunk | while | flops 2 | bytes 393321 | solution.py:51
  189.1 0.6 fusion.65
  189.7 1.3 dynamic-slice.7
  191.0 0.1 copy.48
  191.2 0.6 fusion.65
  191.8 1.3 dynamic-slice.7
  193.1 0.1 copy.48
  193.3 19.7 %custom-call.15 = f32[2,128,128]{1,2,0:T(8,128)S(1)} custom-call(f32[2,128,128]{2,1,0:T(8,128)S(1)} %get-tuple-element.9), custom_call_target="InvertDiagBlocksLowerTriangular" | custom-call | tf_op jit(solution)/shard_map/triangular_solve | solution.py:51
  212.9 0.4 fusion.8
  213.4 0.4 convolution_subtract_fusion
  213.8 0.4 fusion.40
  214.2 7.2 %fusion.6 = f32[256,2048]{1,0:T(8,128)} fusion(f32[512,2048]{1,0:T(8,128)} %param.3, f32[512,128]{0,1:T(8,128)S(1)} %fusion.40, f32[512,128]{0,1:T(8,128)S(1)} %fusion.8), kind=kOutput, calls=%fused_computation.10 | convolution fusion | flops 3221356544 | bytes 6815744 | tf_op jit(solution)/shard_map/dot_general | solution.py:33
  221.4 62.2 %reduce-scatter.2.cloned.1.call-done = f32[16,2048]{1,0:T(8,128)} async-done(((f32[256,2048]{1,0:T(8,128)}), f32[16,2048]{1,0:T(8,128)}) %reduce-scatter.2.cloned.1.call-update) | async-done | bytes 131088 | tf_op jit(solution)/shard_map/reduce_scatter | solution.py:58
  283.6 1.0 reshape.692
  284.6 0.4 copy.32
  285.0 1.5 reshape.713
  286.5 3.4 %all-to-all-start = ((f32[2,1,16384]{2,1,0:T(1,128)}), f32[2,1,16384]{2,1,0:T(1,128)S(1)}, u32[]{:S(2)}, u32[]{:S(2)}) async-start(f32[2,1,16384]{2,1,0:T(1,128)} %reshape.713), calls=%async_computation.1 | async-start | bytes 262144 | tf_op jit(solution)/shard_map/all_to_all | solution.py:62
  289.9 1.0 copy.34
  290.9 3.4 %all-to-all-done = f32[2,1,16384]{2,1,0:T(1,128)S(1)} async-done(((f32[2,1,16384]{2,1,0:T(1,128)}), f32[2,1,16384]{2,1,0:T(1,128)S(1)}, u32[]{:S(2)}, u32[]{:S(2)}) %all-to-all-start) | async-done | bytes 131104 | tf_op jit(solution)/shard_map/all_to_all | solution.py:62
  294.3 0.5 broadcast.1149
  294.8 1.0 reduce.12
  295.9 0.8 reshape.714
  296.6 0.3 copy.33
  297.0 0.7 reshape.693
  (35 shorter events, 0.6 us)
Async XLA Ops:
  7.2 0.7 copy-start
  7.2 49.7 %all-reduce.4.cloned.1.call-start = ((), (), s32[]{:S(2)}) async-start(), calls=%async_computation.2 | async-start | bytes 1048576 | tf_op jit(solution)/shard_map/psum | solution.py:47
  9.5 7.8 %copy-start.1 = (f32[512,2048]{1,0:T(8,128)S(1)}, f32[512,2048]{1,0:T(8,128)}, u32[]{:S(2)}) copy-start(f32[512,2048]{1,0:T(8,128)} %param.3) | copy-start | bytes 12582916
  25.4 124.6 %all-reduce.6.cloned.1.call-start = ((), (), s32[]{:S(2)}) async-start(), calls=%async_computation.3 | async-start | bytes 524288 | tf_op jit(solution)/shard_map/psum | solution.py:48
  59.4 224.2 %reduce-scatter.2.cloned.1.call-start = ((), (), s32[]{:S(2)}) async-start(), calls=%async_computation.4 | async-start | bytes 2228224 | tf_op jit(solution)/shard_map/reduce_scatter | solution.py:58
  163.8 49.1 %copy-start.2 = (f32[512,256]{0,1:T(8,128)S(1)}, f32[512,256]{0,1:T(8,128)}, u32[]{:S(2)}) copy-start(f32[512,256]{0,1:T(8,128)} %all-reduce.4.cloned.1.call-done) | copy-start | bytes 1572868
  286.5 7.8 %all-to-all-start = ((f32[2,1,16384]{2,1,0:T(1,128)}), f32[2,1,16384]{2,1,0:T(1,128)S(1)}, u32[]{:S(2)}, u32[]{:S(2)}) async-start(f32[2,1,16384]{2,1,0:T(1,128)} %reshape.713), calls=%async_computation.1 | async-start | bytes 262144 | tf_op jit(solution)/shard_map/all_to_all | solution.py:62
Sparse Core Ops, SparseCore 0:
  25.5 31.2 all-reduce.3
  61.2 88.7 all-reduce.5
  221.5 62.0 reduce-scatter.1
where the time goes:
time: 305 us; the launch traced here: 304 us
  waiting for transfers between devices  187 us (61%)
  other arithmetic  66.3 us (22%)
  matrix products  19.5 us (6%)
  between operations  15.3 us (5%)
  local copies, waits for them, and re-layouts  11.8 us (4%)
  starting transfers between devices  3.68 us (1%)
    psum x1, waiting for transfers between devices, local(): gram_matrix = lax.psum(inner_rows(sketch, sketch), 'rows')  90.3 us
    reduce_scatter x1, waiting for transfers between devices, local(): lax.psum_scatter(inner_rows(basis_rows, unfolding), 'rows', scatter_dimen...  62.2 us
    another operation x7, other arithmetic, local(): lower_factor = jnp.linalg.cholesky(gram_matrix)  34.6 us
    psum x1, waiting for transfers between devices, local(): sketch = lax.psum(partial_sketch, 'cols')  31.4 us
    another operation x3, other arithmetic, local(): lax.linalg.triangular_solve(lower_factor, sketch, left_side=False, lower=...  19.7 us
    dot_general x2, matrix products, inner_rows(): lax.dot_general(left_side, right_side, (((0,), (0,)), ((), ())), precisio...  9.68 us
    dot_general x1, matrix products, local(): partial_sketch = jnp.dot(unfolding, sketch_map, precision=highest)  8.08 us
    mul x1, other arithmetic, sketch_matrix(): expanded = factor.astype(jnp.float32)[:, :, None] * tiled_table[:, None, :]  7.74 us
  transfers between devices with their start and end apart: 4, of which 4 were waited for; matrix products, arithmetic and copies ran while one was open for 0% of the time, Pallas kernels for 0%

commit v1 on v0

--- a/solution.py
+++ b/solution.py
@@ -3,6 +3,7 @@
 import jax.numpy as jnp
 from jax import lax
 from jax.sharding import PartitionSpec as P
+from jax.lax import all_gather
 
 RANK = 256
 BLK = 128
@@ -45,7 +46,8 @@
     total_rows = local_rows * row_devices
     partial_sketch = jnp.dot(unfolding, sketch_map, precision=highest)
     sketch = lax.psum(partial_sketch, "cols")
-    gram_matrix = lax.psum(inner_rows(sketch, sketch), "rows")
+    arr = inner_rows(sketch, sketch)
+    gram_matrix = all_gather(arr, "rows").sum(axis=0)
     gram_matrix = gram_matrix + float(total_rows) * jnp.eye(RANK, dtype=jnp.float32)
     lower_factor = jnp.linalg.cholesky(gram_matrix)
     basis_rows = lax.linalg.triangular_solve(

time: 305 us -> 263 us (0.86)
  waiting for transfers between devices: 187 us -> 146 us
    psum x1 -> x0, waiting for transfers between devices: 90.3 us -> none  [local(): gram_matrix = lax.psum(inner_rows(sketch, sketch), 'rows')]
    all_gather x0 -> x1, waiting for transfers between devices: none -> 50.9 us  [local(): gram_matrix = all_gather(arr, 'rows').sum(axis=0)]
where the time goes in v1:
time: 263 us
  waiting for transfers between devices  146 us (56%)
  other arithmetic  66.8 us (25%)
  matrix products  19.4 us (7%)
  between operations  15.3 us (6%)
  local copies, waits for them, and re-layouts  11.4 us (4%)
  starting transfers between devices  3.68 us (1%)
    reduce_scatter x1, waiting for transfers between devices, local(): lax.psum_scatter(inner_rows(basis_rows, unfolding), 'rows', scatter_dimen...  60.2 us
    all_gather x1, waiting for transfers between devices, local(): gram_matrix = all_gather(arr, 'rows').sum(axis=0)  50.9 us
    another operation x7, other arithmetic, local(): lower_factor = jnp.linalg.cholesky(gram_matrix)  34.6 us
    psum x1, waiting for transfers between devices, local(): sketch = lax.psum(partial_sketch, 'cols')  31.4 us
    another operation x3, other arithmetic, local(): lax.linalg.triangular_solve(lower_factor, sketch, left_side=False, lower=...  19.7 us
    dot_general x2, matrix products, inner_rows(): lax.dot_general(left_side, right_side, (((0,), (0,)), ((), ())), precisio...  9.67 us
    dot_general x1, matrix products, local(): partial_sketch = jnp.dot(unfolding, sketch_map, precision=highest)  8.08 us
    mul x1, other arithmetic, sketch_matrix(): expanded = factor.astype(jnp.float32)[:, :, None] * tiled_table[:, None, :]  7.74 us
  transfers between devices with their start and end apart: 4, of which 4 were waited for; matrix products, arithmetic and copies ran while one was open for 0% of the time, Pallas kernels for 0%

profile of v1, /device:TPU:0, one launch (start us, length us, event | category | flops | bytes accessed | tf_op | source)
XLA Modules:
  0.0 262.8 jit_solution(6539153903838008490)
XLA Ops:
  7.2 0.0 all-reduce.3.cloned.1.call-start
  7.3 0.5 copy-done
  7.8 0.1 broadcast_bitcast_fusion
  7.9 0.7 fusion.50
  8.7 0.4 copy.14
  9.0 0.4 fusion.26
  9.4 0.1 tile.8
  9.5 7.7 %broadcast_multiply_fusion = f32[2048,2,128]{2,1,0:T(2,128)S(1)} fusion(f32[2048,128]{1,0:T(8,128)S(1)} %bitcast.59, f32[2048,2]{1,0:T(8,128)S(1)} %copy.14), kind=kLoop, calls=%fused_computation.8 | loop fusion | flops 524288 | bytes 3162112 | tf_op jit(solution)/shard_map/mul | solution.py:29
  17.3 8.1 %fusion.3 = f32[512,256]{0,1:T(8,128)} fusion(f32[512,2048]{1,0:T(8,128)S(1)} %copy-done.1, f32[256,8,2,128]{3,2,1,0:T(2,128)S(1)} %bitcast.55), kind=kOutput, calls=%fused_computation.5 | convolution fusion | flops 3221225472 | bytes 6815744 | tf_op jit(solution)/shard_map/dot_general | solution.py:47
  25.4 0.0 all-gather.3.cloned.1.call-start
  25.5 31.4 %all-reduce.3.cloned.1.call-done = f32[512,256]{0,1:T(8,128)} async-done(((f32[512,256]{0,1:T(8,128)}), f32[512,256]{0,1:T(8,128)}) %all-reduce.3.cloned.1.call-update) | async-done | bytes 524304 | tf_op jit(solution)/shard_map/psum | solution.py:48
  56.9 2.5 fusion.54
  59.4 0.2 reduce-scatter.2.cloned.1.call-start
  59.7 50.9 %all-gather.3.cloned.1.call-done = f32[4096,256]{1,0:T(8,128)} async-done(((f32[256,256]{1,0:T(8,128)}), f32[4096,256]{1,0:T(8,128)}) %all-gather.3.cloned.1.call-update) | async-done | bytes 4194320 | tf_op jit(solution)/shard_map/all_gather | solution.py:50
  110.6 2.5 reduce_sum.11
  113.1 0.1 copy.15
  113.2 0.1 add_multiply_fusion
  113.3 11.7 %cholesky.45 = f32[128,128]{1,0:T(8,128)S(1)} custom-call(f32[128,128]{1,0:T(8,128)S(1)} %cholesky.107), custom_call_target="Cholesky" | custom-call | tf_op jit(solution)/shard_map/jit(cholesky)/cholesky | solution.py:52
  125.1 9.8 %custom-call.14 = f32[1,128,128]{1,2,0:T(8,128)S(1)} custom-call(f32[1,128,128]{2,1,0:T(8,128)S(1)} %get-tuple-element.29), custom_call_target="InvertDiagBlocksLowerTriangular" | custom-call | tf_op jit(solution)/shard_map/jit(cholesky)/cholesky | solution.py:52
  134.9 0.2 constant_dynamic-update-slice_fusion.1
  135.1 0.3 convolution_subtract_fusion.1
  135.3 11.7 %cholesky.95 = f32[128,128]{1,0:T(8,128)S(1)} custom-call(f32[128,128]{1,0:T(8,128)S(1)} %convolution_subtract_fusion.1), custom_call_target="Cholesky" | custom-call | tf_op jit(solution)/shard_map/jit(cholesky)/cholesky | solution.py:52
  147.1 0.7 compare_reduce_fusion
  147.7 0.6 compare_reduce_fusion.1
  149.7 0.1 triangular_solve.64
  149.8 4.1 %while.1 = (s32[]{:T(128)}, f32[256,256]{1,0:T(8,128)S(1)}, s32[2,2]{1,0:T(2,128)S(1)}, f32[2,128,128]{2,1,0:T(8,128)S(1)}, s32[]{:T(128)}) while((s32[]{:T(128)}, f32[256,256]{1,0:T(8,128)S(1)}, s32[2,2]{1,0:T(2,128)S(1)}, f32[2,128,128]{2,1,0:T(8,128)S(1)}, s32[]{:T(128)}) %tuple.38), condition=%wide.while_cond, body=%wide.while_body.sunk | while | flops 2 | bytes 131181 | solution.py:53
  149.9 0.6 fusion.64
  150.5 1.4 bitcast_dynamic-update-slice_fusion.2
  151.9 0.6 fusion.64
  152.5 1.4 bitcast_dynamic-update-slice_fusion.2
  153.9 19.7 %custom-call.15 = f32[2,128,128]{1,2,0:T(8,128)S(1)} custom-call(f32[2,128,128]{2,1,0:T(8,128)S(1)} %get-tuple-element.9), custom_call_target="InvertDiagBlocksLowerTriangular" | custom-call | tf_op jit(solution)/shard_map/triangular_solve | solution.py:53
  173.6 0.4 fusion.8
  174.0 0.4 convolution_subtract_fusion
  174.4 0.4 fusion.39
  174.8 7.1 %fusion.6 = f32[256,2048]{1,0:T(8,128)} fusion(f32[512,2048]{1,0:T(8,128)} %param.3, f32[512,128]{0,1:T(8,128)S(1)} %fusion.39, f32[512,128]{0,1:T(8,128)S(1)} %fusion.8), kind=kOutput, calls=%fused_computation.10 | convolution fusion | flops 3221356544 | bytes 6815744 | tf_op jit(solution)/shard_map/dot_general | solution.py:34
  182.0 60.2 %reduce-scatter.2.cloned.1.call-done = f32[16,2048]{1,0:T(8,128)} async-done(((f32[256,2048]{1,0:T(8,128)}), f32[16,2048]{1,0:T(8,128)}) %reduce-scatter.2.cloned.1.call-update) | async-done | bytes 131088 | tf_op jit(solution)/shard_map/reduce_scatter | solution.py:60
  242.2 1.0 reshape.692
  243.2 0.4 copy.17
  243.6 1.5 reshape.714
  245.1 3.4 %all-to-all-start = ((f32[2,1,16384]{2,1,0:T(1,128)}), f32[2,1,16384]{2,1,0:T(1,128)S(1)}, u32[]{:S(2)}, u32[]{:S(2)}) async-start(f32[2,1,16384]{2,1,0:T(1,128)} %reshape.714), calls=%async_computation.1 | async-start | bytes 262144 | tf_op jit(solution)/shard_map/all_to_all | solution.py:64
  248.5 0.1 fusion.7
  248.5 1.0 copy.19
  249.5 3.4 %all-to-all-done = f32[2,1,16384]{2,1,0:T(1,128)S(1)} async-done(((f32[2,1,16384]{2,1,0:T(1,128)}), f32[2,1,16384]{2,1,0:T(1,128)S(1)}, u32[]{:S(2)}, u32[]{:S(2)}) %all-to-all-start) | async-done | bytes 131104 | tf_op jit(solution)/shard_map/all_to_all | solution.py:64
  252.9 0.5 broadcast.1149
  253.4 1.0 reduce.12
  254.4 0.8 reshape.715
  255.2 0.3 copy.18
  255.5 0.7 reshape.693
  (26 shorter events, 0.3 us)
Async XLA Ops:
  7.2 0.7 copy-start
  7.2 49.7 %all-reduce.3.cloned.1.call-start = ((), (), s32[]{:S(2)}) async-start(), calls=%async_computation.2 | async-start | bytes 1048576 | tf_op jit(solution)/shard_map/psum | solution.py:48
  9.5 7.8 %copy-start.1 = (f32[512,2048]{1,0:T(8,128)S(1)}, f32[512,2048]{1,0:T(8,128)}, u32[]{:S(2)}) copy-start(f32[512,2048]{1,0:T(8,128)} %param.3) | copy-start | bytes 12582916
  25.4 85.2 %all-gather.3.cloned.1.call-start = ((), (), s32[]{:S(2)}) async-start(), calls=%async_computation.4 | async-start | bytes 4456448 | tf_op jit(solution)/shard_map/all_gather | solution.py:50
  59.4 182.8 %reduce-scatter.2.cloned.1.call-start = ((), (), s32[]{:S(2)}) async-start(), calls=%async_computation.3 | async-start | bytes 2228224 | tf_op jit(solution)/shard_map/reduce_scatter | solution.py:60
  113.1 60.5 %copy-start.2 = (f32[512,256]{0,1:T(8,128)S(1)}, f32[512,256]{0,1:T(8,128)}, u32[]{:S(2)}) copy-start(f32[512,256]{0,1:T(8,128)} %all-reduce.3.cloned.1.call-done) | copy-start | bytes 1572868
  245.1 7.8 %all-to-all-start = ((f32[2,1,16384]{2,1,0:T(1,128)}), f32[2,1,16384]{2,1,0:T(1,128)S(1)}, u32[]{:S(2)}, u32[]{:S(2)}) async-start(f32[2,1,16384]{2,1,0:T(1,128)} %reshape.714), calls=%async_computation.1 | async-start | bytes 262144 | tf_op jit(solution)/shard_map/all_to_all | solution.py:64
Sparse Core Ops, SparseCore 0:
  25.5 31.2 all-reduce.2
  59.8 50.7 all-gather.2
  182.1 60.0 reduce-scatter.1
